TPU v7x, 32 devices: a whole 2x2x4 slice. The times are simulated.
32 devices in a mesh: groups: 2 (over y), emit: 4 (over z), recv: 4 (over x, core).
Axes of the slice: x: 2, y: 2, z: 4, core: 2. Of those that a mesh axis runs over, the one named last changes fastest.
Arguments:
- positions: float32 [3, 8192], P(None, ('groups', 'emit', 'recv')), parts along dimension 1, may hold values from 0 to 1
- angles: float32 [2, 8192], P(None, ('groups', 'emit', 'recv')), parts along dimension 1, may hold values from -3.140625 to 3.140625
- areas: float32 [8192], P(('groups', 'emit', 'recv')), parts along dimension 0, may hold values from 0.00024414062 to 0.00390625
- emissivity: float32 [8192], P(('groups', 'emit', 'recv')), parts along dimension 0, may hold values from 0.1 to 0.9
- emission: float32 [32, 8192], P(None, ('groups', 'emit', 'recv')), parts along dimension 1, may hold values from 0.5 to 2
- radiosity_in: float32 [32, 8192], P(None, ('groups', 'emit', 'recv')), parts along dimension 1, may hold values from 0.2 to 2
- adjoint_in: float32 [32, 8192], P(None, ('groups', 'emit', 'recv')), parts along dimension 1, may hold values from 0 to 1.5
- visibility: int32 [64, 32], P(('groups', 'emit')), parts along dimension 0, may hold values 0 or 1
- inlet_patches: int32 [4096], P('groups'), parts along dimension 0, may hold values from 0 to 4095
- inlet_weights: float32 [32, 4096], P(None, 'groups'), parts along dimension 1, may hold values from 0.5 to 2
Outputs:
- radiosity_out: float32 [32, 8192], P(None, ('groups', 'emit', 'recv')), parts along dimension 1
- adjoint_out: float32 [32, 8192], P(None, ('groups', 'emit', 'recv')), parts along dimension 1
- emissivity_grad: float32 [8192], P(('groups', 'emit', 'recv')), parts along dimension 0
There are 2 independent parts, one for each index of `groups`. A program takes and returns all parts, laid end to end along the dimension named above; each array names one. Nothing has to cross between parts.
Inputs may be any that keep to these rules, and one draw needn't show every extreme that they name: `inlet_patches`: an inlet patch may be listed more than once.
All inputs are finite; a program needn't handle non-finite values. No bound on the sum of `visibility` on one device may be relied on, other than what follows from the above.
Results may differ from a plain program's by a relative error of at most 0.0003.
Values may be sent and summed in bfloat16 or wider, within the bound.
No kernel may reach another device: no remote copies, remote signals or barrier semaphores. Data moves between devices by JAX's collectives and lax.ppermute only.
A program may use at most 64 MiB of HBM per device.

v0:
```python
import math
import jax
import jax.numpy as jnp
from jax import lax
from jax.sharding import PartitionSpec as P

BLK = 128


def patch_geometry(positions, angles, areas):
    polar = angles[0]
    azimuth = angles[1]
    normal = jnp.stack(
        [jnp.sin(polar) * jnp.cos(azimuth), jnp.sin(polar) * jnp.sin(azimuth), jnp.cos(polar)]
    )
    return jnp.concatenate([positions, normal, areas[None, :]], axis=0)


def view_tile(row_geom, col_geom, block_mask):
    delta_x = col_geom[0][None, :] - row_geom[0][:, None]
    delta_y = col_geom[1][None, :] - row_geom[1][:, None]
    delta_z = col_geom[2][None, :] - row_geom[2][:, None]
    dist_sq = delta_x * delta_x + delta_y * delta_y + delta_z * delta_z
    cos_emit = jnp.maximum(
        row_geom[3][:, None] * delta_x
        + row_geom[4][:, None] * delta_y
        + row_geom[5][:, None] * delta_z,
        0.0,
    )
    cos_recv = jnp.maximum(
        -(
            col_geom[3][None, :] * delta_x
            + col_geom[4][None, :] * delta_y
            + col_geom[5][None, :] * delta_z
        ),
        0.0,
    )
    patch_area = row_geom[6][:, None]
    spread = dist_sq + patch_area
    kernel = cos_emit * cos_recv * patch_area / (math.pi * spread * spread)
    row_blocks, col_blocks = block_mask.shape
    rows_total = row_geom.shape[1]
    cols_total = col_geom.shape[1]
    expanded = jnp.broadcast_to(
        block_mask[:, None, :, None],
        (row_blocks, rows_total // row_blocks, col_blocks, cols_total // col_blocks),
    ).reshape(rows_total, cols_total)
    return (expanded * kernel).astype(jnp.bfloat16)


def block_width():
    return 128


def local(
    positions,
    angles,
    areas,
    emissivity,
    emission,
    radiosity_in,
    adjoint_in,
    visibility,
    inlet_patches,
    inlet_weights,
):
    emit_count = lax.axis_size("emit")
    recv_count = lax.axis_size("recv")
    emit_index = lax.axis_index("emit")
    recv_index = lax.axis_index("recv")
    own_count = areas.shape[0]
    cases = emission.shape[0]
    geometry = patch_geometry(positions, angles, areas)
    reflect = 1.0 - emissivity
    own_weights = (reflect[None, :] * adjoint_in).astype(jnp.bfloat16)
    own_values = radiosity_in.astype(jnp.bfloat16)
    mask_rows = visibility.shape[0]
    per_block = visibility.shape[1] // emit_count
    own_blocks = own_count // BLK
    folded_mask = visibility.astype(jnp.float32).reshape(mask_rows, emit_count, per_block)
    tile_mask = lax.dynamic_slice_in_dim(
        folded_mask, recv_index * own_blocks, own_blocks, 2
    ).reshape(mask_rows, emit_count * own_blocks)
    row_total = own_count * recv_count
    col_total = own_count * emit_count
    row_values = lax.all_gather(own_values, "recv", axis=1, tiled=True)
    col_weight = lax.all_gather(own_weights, "emit", axis=1, tiled=True)
    start_state = (
        jnp.zeros((cases, col_total), jnp.float32),
        jnp.zeros((cases, row_total), jnp.float32),
    )
    col_geom = lax.all_gather(geometry, "emit", axis=1, tiled=True)
    geom_piece = lax.all_gather(geometry, "recv", axis=1, tiled=True)
    count = geom_piece.shape[1]
    width = block_width()

    def inner(number, state):
        fwd_total, adj_total = state
        offset = number * width
        geom_part = lax.dynamic_slice_in_dim(geom_piece, offset, width, 1)
        value_part = lax.dynamic_slice_in_dim(row_values, offset, width, 1)
        mask_part = lax.dynamic_slice_in_dim(tile_mask, offset // BLK, width // BLK, 0)
        tile = view_tile(geom_part, col_geom, mask_part)
        fwd_total = fwd_total + jnp.dot(value_part, tile, preferred_element_type=jnp.float32)
        adj_part = lax.dot_general(
            col_weight, tile, (((1,), (1,)), ((), ())), preferred_element_type=jnp.float32
        )
        adj_total = lax.dynamic_update_slice_in_dim(adj_total, adj_part, offset, 1)
        return (fwd_total, adj_total)

    forward, adjoint = lax.fori_loop(0, count // width, inner, start_state)
    incoming = lax.psum_scatter(forward, "emit", scatter_dimension=1, tiled=True)
    returned = lax.psum_scatter(adjoint, "recv", scatter_dimension=1, tiled=True)
    own_ids = (emit_index * recv_count + recv_index) * own_count + lax.iota(jnp.int32, own_count)
    selector = (inlet_patches[:, None] == own_ids[None, :]).astype(jnp.float32)
    source = jnp.dot(
        inlet_weights, selector, precision=lax.Precision.HIGHEST, preferred_element_type=jnp.float32
    )
    radiosity_out = emissivity[None, :] * emission + reflect[None, :] * incoming
    adjoint_out = source + returned
    emissivity_grad = jnp.sum(adjoint_out * (emission - incoming), axis=0)
    return (radiosity_out, adjoint_out, emissivity_grad)


def solution(mesh):
    placed = (
        P(None, ("groups", "emit", "recv")),
        P(None, ("groups", "emit", "recv")),
        P(("groups", "emit", "recv")),
        P(("groups", "emit", "recv")),
        P(None, ("groups", "emit", "recv")),
        P(None, ("groups", "emit", "recv")),
        P(None, ("groups", "emit", "recv")),
        P(("groups", "emit"), None),
        P("groups"),
        P(None, "groups"),
    )
    return jax.shard_map(
        local,
        mesh=mesh,
        in_specs=placed,
        out_specs=(
            P(None, ("groups", "emit", "recv")),
            P(None, ("groups", "emit", "recv")),
            P(("groups", "emit", "recv")),
        ),
        check_vma=False,
    )
```

profile of v0, /device:TPU:0, one launch (start us, length us, event | category | flops | bytes accessed | tf_op | source)
XLA Modules:
  0.0 115.8 jit_solution(4974398801967030085)
XLA Ops:
  7.2 0.0 copy-start
  7.2 0.0 reduce-scatter.5.cloned.1.call-start
  7.2 0.8 slice_cosine_fusion
  8.1 0.7 concatenate.3
  8.8 14.8 %all_gather.14 = f32[7,1024]{1,0:T(8,128)S(1)} all-gather(f32[7,256]{1,0:T(8,128)S(1)} %concatenate.3), channel_id=1, replica_groups=mesh['groups'=2,'emit'=4,'recv'=4] {'emit'}, dimensions={1}, use_global_device_ids=true | all-gather | bytes 35840 | tf_op jit(solution)/shard_map/all_gather | solution.py:92
  23.6 5.2 %all_gather.13 = f32[7,1024]{1,0:T(8,128)S(1)} all-gather(f32[7,256]{1,0:T(8,128)S(1)} %concatenate.3), channel_id=1, replica_groups=mesh['groups'=2,'emit'=4,'recv'=4] {'recv'}, dimensions={1}, use_global_device_ids=true | all-gather | bytes 35840 | tf_op jit(solution)/shard_map/all_gather | solution.py:93
  28.8 0.7 broadcast_subtract_fusion
  29.5 0.7 convert_element_type.21
  30.1 0.1 copy.15
  30.2 0.1 copy.14
  30.3 0.8 convert_element_type.20
  31.1 5.2 %all_gather.12 = bf16[32,1024]{1,0:T(8,128)(2,1)S(1)} all-gather(bf16[32,256]{1,0:T(8,128)(2,1)S(1)} %convert_element_type.20), channel_id=1, replica_groups=mesh['groups'=2,'emit'=4,'recv'=4] {'recv'}, dimensions={1}, use_global_device_ids=true | all-gather | bytes 81920 | tf_op jit(solution)/shard_map/all_gather | solution.py:86
  36.3 13.1 %all_gather.15 = bf16[32,1024]{1,0:T(8,128)(2,1)S(1)} all-gather(bf16[32,256]{1,0:T(8,128)(2,1)S(1)} %multiply_convert_fusion), channel_id=1, replica_groups=mesh['groups'=2,'emit'=4,'recv'=4] {'emit'}, dimensions={1}, use_global_device_ids=true | all-gather | bytes 81920 | tf_op jit(solution)/shard_map/all_gather | solution.py:87
  49.4 13.7 %while.18 = (s32[]{:T(128)}, f32[32,1024]{1,0:T(8,128)S(1)}, f32[32,1024]{1,0:T(8,128)S(1)}, bf16[32,1024]{1,0:T(8,128)(2,1)S(1)}, f32[8,8]{1,0:T(8,128)S(1)}, /...) while((s32[]{:T(128)}, f32[32,1024]{1,0:T(8,128)S(1)}, ...), condition=%wide.region_1.2_spmd.clone, body=%wide.region_0.1_spmd.clone.sunk | while | flops 24444952 | bytes 484852 | solution.py:111
  49.5 0.1 broadcast_bitcast_fusion.2
  49.6 0.8 convolution_add_fusion.2
  50.4 0.8 fusion.47
  51.2 0.1 broadcast_bitcast_fusion.2
  51.3 0.8 convolution_add_fusion.2
  52.1 0.8 fusion.47
  52.9 0.1 broadcast_bitcast_fusion.2
  53.0 0.8 convolution_add_fusion.2
  53.8 0.8 fusion.47
  54.6 0.1 broadcast_bitcast_fusion.2
  54.7 0.8 convolution_add_fusion.2
  55.5 0.8 fusion.47
  56.3 0.1 broadcast_bitcast_fusion.2
  56.4 0.8 convolution_add_fusion.2
  57.2 0.8 fusion.47
  58.0 0.1 broadcast_bitcast_fusion.2
  58.1 0.8 convolution_add_fusion.2
  58.9 0.8 fusion.47
  59.7 0.1 broadcast_bitcast_fusion.2
  59.8 0.8 convolution_add_fusion.2
  60.6 0.8 fusion.47
  61.4 0.1 broadcast_bitcast_fusion.2
  61.5 0.8 convolution_add_fusion.2
  62.4 0.8 fusion.47
  63.1 0.0 copy-start.1
  63.2 0.0 copy-start.5
  63.2 0.0 copy-start.6
  63.2 0.6 copy-done.1
  63.8 0.0 reduce-scatter.5.cloned.1.call-update
  63.8 0.0 reduce-scatter.3.cloned.1.call-start
  63.9 0.7 reduce-scatter.3.cloned.1.call-update
  64.6 20.0 %reduce-scatter.5.cloned.1.call-done = f32[32,256]{1,0:T(8,128)} async-done(((f32[32,1024]{1,0:T(8,128)}), f32[32,256]{1,0:T(8,128)}) %reduce-scatter.5.cloned.1.call-update) | async-done | bytes 32784 | tf_op jit(solution)/shard_map/reduce_scatter | solution.py:113
  84.6 21.6 %reduce-scatter.3.cloned.1.call-done = f32[32,256]{1,0:T(8,128)} async-done(((f32[32,1024]{1,0:T(8,128)}), f32[32,256]{1,0:T(8,128)}) %reduce-scatter.3.cloned.1.call-update) | async-done | bytes 32784 | tf_op jit(solution)/shard_map/reduce_scatter | solution.py:112
  106.2 2.8 %multiply_reduce_fusion = (f32[256]{0:T(256)}, f32[32,256]{1,0:T(8,128)}, f32[32,256]{1,0:T(8,128)}) fusion(f32[32,256]{1,0:T(8,128)S(1)} %copy-done.5, f32[32,256]{1,0:T(8,128)} %reduce-scatter.3.cloned.1.call-done, f32[256]{0:T(256)S(1)} %broadcast_subtract_fusion, f32[256]{0:T(256)S(1)} %copy-done.4, f32[32,256]{1,0:T(8,128)} %reduce-scatter.5.cloned.1.call-done, ...), kind=kOutput, calls=%fused_computation.47 | convolution fusion | flops 201907968 | bytes 438272 | tf_op jit(solution)/shard_map/dot_general | solution.py:116
  (46 shorter events, 0.4 us)
Async XLA Ops:
  7.2 99.0 %copy-start = (f32[32,2048]{1,0:T(8,128)S(1)}, f32[32,2048]{1,0:T(8,128)}, u32[]{:S(2)}) copy-start(f32[32,2048]{1,0:T(8,128)} %param.21) | copy-start | bytes 786436
  7.2 29.1 %copy-start.3 = (f32[32,256]{1,0:T(8,128)S(1)}, f32[32,256]{1,0:T(8,128)}, u32[]{:S(2)}) copy-start(f32[32,256]{1,0:T(8,128)} %param.18) | copy-start | bytes 98308
  7.2 77.4 %reduce-scatter.5.cloned.1.call-start = ((), (), s32[]{:S(2)}) async-start(), calls=%async_computation.3 | async-start | bytes 163840 | tf_op jit(solution)/shard_map/reduce_scatter | solution.py:113
  63.1 0.7 copy-start.1
  63.1 0.7 copy-start.2
  63.1 43.0 %copy-start.4 = (f32[256]{0:T(256)S(1)}, f32[256]{0:T(256)}, u32[]{:S(2)}) copy-start(f32[256]{0:T(256)} %param.15) | copy-start | bytes 3076
  63.2 43.0 %copy-start.5 = (f32[32,256]{1,0:T(8,128)S(1)}, f32[32,256]{1,0:T(8,128)}, u32[]{:S(2)}) copy-start(f32[32,256]{1,0:T(8,128)} %param.16) | copy-start | bytes 98308
  63.2 43.0 %copy-start.6 = (s32[2048]{0:T(1024)S(1)}, s32[2048]{0:T(1024)}, u32[]{:S(2)}) copy-start(s32[2048]{0:T(1024)} %param.20) | copy-start | bytes 24580
  63.8 42.3 %reduce-scatter.3.cloned.1.call-start = ((), (), s32[]{:S(2)}) async-start(), calls=%async_computation.2 | async-start | bytes 163840 | tf_op jit(solution)/shard_map/reduce_scatter | solution.py:112
Sparse Core Ops, SparseCore 0:
  63.9 20.5 reduce-scatter.4
  86.9 19.1 reduce-scatter.2
where the time goes:
time: 116 us
  waiting for transfers between devices  42.3 us (36%)
  blocking collectives  38.3 us (33%)
  matrix products  15.3 us (13%)
  between operations  14.1 us (12%)
  other arithmetic  2.97 us (3%)
  local copies, waits for them, and re-layouts  2.42 us (2%)
    reduce_scatter x1, waiting for transfers between devices, local(): lax.psum_scatter(forward, 'emit', scatter_dimension=1, tiled=True)  21.6 us
    reduce_scatter x1, waiting for transfers between devices, local(): lax.psum_scatter(adjoint, 'recv', scatter_dimension=1, tiled=True)  20 us
    all_gather x1, blocking collectives, local(): col_geom = lax.all_gather(geometry, 'emit', axis=1, tiled=True)  14.8 us
    all_gather x1, blocking collectives, local(): col_weight = lax.all_gather(own_weights, 'emit', axis=1, tiled=True)  13.1 us
    dot_general x8, matrix products, inner(): jnp.dot(value_part, tile, preferred_element_type=jnp.float32)  6.43 us
    dot_general x8, matrix products, inner(): lax.dot_general(col_weight, tile, (((1,), (1,)), ((), ())), preferred_ele...  6.15 us
    all_gather x1, blocking collectives, local(): row_values = lax.all_gather(own_values, 'recv', axis=1, tiled=True)  5.23 us
    all_gather x1, blocking collectives, local(): geom_piece = lax.all_gather(geometry, 'recv', axis=1, tiled=True)  5.18 us
  transfers between devices with their start and end apart: 2, of which 2 were waited for; matrix products, arithmetic and copies ran while one was open for 0% of the time, Pallas kernels for 0%

commit v1 on v0

--- a/solution.py
+++ b/solution.py
@@ -5,6 +5,18 @@
 from jax.sharding import PartitionSpec as P
 
 BLK = 128
+
+
+def collect(value, axis, dim):
+    ways, here, step = (lax.axis_size(axis), lax.axis_index(axis), value.shape[dim])
+    lengths = [n * ways if d == dim else n for d, n in enumerate(value.shape)]
+    full = lax.dynamic_update_slice_in_dim(
+        jnp.zeros(lengths, value.dtype), value, here * step, axis=dim
+    )
+    for far in range(1, ways):
+        value = lax.ppermute(value, axis, [(d, (d + 1) % ways) for d in range(ways)])
+        full = lax.dynamic_update_slice_in_dim(full, value, (here - far) % ways * step, axis=dim)
+    return full
 
 
 def patch_geometry(positions, angles, areas):
@@ -84,7 +96,7 @@
     row_total = own_count * recv_count
     col_total = own_count * emit_count
     row_values = lax.all_gather(own_values, "recv", axis=1, tiled=True)
-    col_weight = lax.all_gather(own_weights, "emit", axis=1, tiled=True)
+    col_weight = collect(own_weights, "emit", 1)
     start_state = (
         jnp.zeros((cases, col_total), jnp.float32),
         jnp.zeros((cases, row_total), jnp.float32),

time: 116 us -> 109 us (0.940)
  blocking collectives: 38.3 us -> 23.8 us
  waiting for transfers between devices: 42.3 us -> 48 us
  starting transfers between devices: 0.08 us -> 3.12 us
  matrix products: 15.3 us -> 13.4 us
  other arithmetic: 2.97 us -> 4.22 us
    all_gather x1 -> x0, blocking collectives: 13.1 us -> none  [local(): col_weight = lax.all_gather(own_weights, 'emit', axis=1, tiled=True)]
    ppermute x0 -> x3, waiting for transfers between devices: none -> 11.1 us  [collect(): lax.ppermute(value, axis, [(d, (d + 1) % ways) for d in range(ways)])]
    reduce_scatter x1, waiting for transfers between devices: 21.6 us -> 15.9 us  [local(): lax.psum_scatter(forward, 'emit', scatter_dimension=1, tiled=True)]
    ppermute x0 -> x3, starting transfers between devices: none -> 3.04 us  [collect(): lax.ppermute(value, axis, [(d, (d + 1) % ways) for d in range(ways)])]
    reduce_sum x0 -> x1, other arithmetic: none -> 1.97 us  [local(): emissivity_grad = jnp.sum(adjoint_out * (emission - incoming), axis=0)]
    dot_general x1, matrix products: 2.76 us -> 0.8 us  [local(): jnp.dot(inlet_weights, selector, precision=lax.Precision.HIGHEST, preferr...]
    all_gather x1, blocking collectives: 14.8 us -> 13.3 us  [local(): col_geom = lax.all_gather(geometry, 'emit', axis=1, tiled=True)]
  transfers between devices with their start and end apart: 2 -> 5, of which waited for: 2 -> 4; matrix products, arithmetic and copies ran while one was open for 0% -> 2% of each run, Pallas kernels for 0% -> 0%
where the time goes in v1:
time: 109 us
  waiting for transfers between devices  48 us (44%)
  blocking collectives  23.8 us (22%)
  between operations  14.2 us (13%)
  matrix products  13.4 us (12%)
  other arithmetic  4.22 us (4%)
  starting transfers between devices  3.12 us (3%)
  local copies, waits for them, and re-layouts  1.73 us (2%)
    reduce_scatter x1, waiting for transfers between devices, local(): lax.psum_scatter(adjoint, 'recv', scatter_dimension=1, tiled=True)  20.3 us
    reduce_scatter x1, waiting for transfers between devices, local(): lax.psum_scatter(forward, 'emit', scatter_dimension=1, tiled=True)  15.9 us
    all_gather x1, blocking collectives, local(): col_geom = lax.all_gather(geometry, 'emit', axis=1, tiled=True)  13.3 us
    ppermute x3, waiting for transfers between devices, collect(): lax.ppermute(value, axis, [(d, (d + 1) % ways) for d in range(ways)])  11.1 us
    dot_general x8, matrix products, inner(): jnp.dot(value_part, tile, preferred_element_type=jnp.float32)  6.43 us
    dot_general x8, matrix products, inner(): lax.dot_general(col_weight, tile, (((1,), (1,)), ((), ())), preferred_ele...  6.12 us
    all_gather x1, blocking collectives, local(): row_values = lax.all_gather(own_values, 'recv', axis=1, tiled=True)  5.25 us
    all_gather x1, blocking collectives, local(): geom_piece = lax.all_gather(geometry, 'recv', axis=1, tiled=True)  5.19 us
  transfers between devices with their start and end apart: 5, of which 4 were waited for; matrix products, arithmetic and copies ran while one was open for 2% of the time, Pallas kernels for 0%

profile of v1, /device:TPU:0, one launch (start us, length us, event | category | flops | bytes accessed | tf_op | source)
XLA Modules:
  0.0 109.0 jit_solution(10122373222317811540)
XLA Ops:
  7.2 0.0 copy-start
  7.2 0.0 reduce-scatter.3.cloned.1.call-start
  7.3 0.7 broadcast_subtract_fusion
  8.0 0.8 constant_dynamic-update-slice_fusion.3
  8.8 3.0 %collective-permute-start = (bf16[32,256]{1,0:T(8,128)(2,1)S(1)}, bf16[32,256]{1,0:T(8,128)(2,1)S(1)}, u32[]{:S(2)}, u32[]{:S(2)}) collective-permute-start(bf16[32,256]{1,0:T(8,128)(2,1)S(1)} %get-tuple-element.259), channel_id=1, source_target_pairs={{0,4},{4,8},{8,12},{12,0},{1,5},{5,9},{9,13},{13,1},{2,6},{6,10},{... | collective-permute-start | bytes 49160 | tf_op jit(solution)/shard_map/ppermute | solution.py:17
  11.8 0.7 convert_element_type.21
  12.5 0.1 copy.15
  12.6 0.1 copy.14
  12.6 0.1 slice_cosine_fusion
  12.7 5.2 %all_gather.9 = bf16[32,1024]{1,0:T(8,128)(2,1)S(1)} all-gather(bf16[32,256]{1,0:T(8,128)(2,1)S(1)} %convert_element_type.20), channel_id=1, replica_groups=mesh['groups'=2,'emit'=4,'recv'=4] {'recv'}, dimensions={1}, use_global_device_ids=true | all-gather | bytes 81920 | tf_op jit(solution)/shard_map/all_gather | solution.py:98
  18.0 5.2 %all_gather.10 = f32[7,1024]{1,0:T(8,128)S(1)} all-gather(f32[7,256]{1,0:T(8,128)S(1)} %concatenate.3), channel_id=1, replica_groups=mesh['groups'=2,'emit'=4,'recv'=4] {'recv'}, dimensions={1}, use_global_device_ids=true | all-gather | bytes 35840 | tf_op jit(solution)/shard_map/all_gather | solution.py:105
  23.2 13.3 %all_gather.11 = f32[7,1024]{1,0:T(8,128)S(1)} all-gather(f32[7,256]{1,0:T(8,128)S(1)} %concatenate.3), channel_id=1, replica_groups=mesh['groups'=2,'emit'=4,'recv'=4] {'emit'}, dimensions={1}, use_global_device_ids=true | all-gather | bytes 35840 | tf_op jit(solution)/shard_map/all_gather | solution.py:104
  36.6 0.0 collective-permute-start.1
  36.6 5.5 %collective-permute-done.1 = bf16[32,256]{1,0:T(8,128)(2,1)S(1)} collective-permute-done((bf16[32,256]{1,0:T(8,128)(2,1)S(1)}, bf16[32,256]{1,0:T(8,128)(2,1)S(1)}, u32[]{:S(2)}, u32[]{:S(2)}) %collective-permute-start.1) | collective-permute-done | bytes 16416 | tf_op jit(solution)/shard_map/ppermute | solution.py:17
  42.1 5.5 %collective-permute-done.2 = bf16[32,256]{1,0:T(8,128)(2,1)S(1)} collective-permute-done((bf16[32,256]{1,0:T(8,128)(2,1)S(1)}, bf16[32,256]{1,0:T(8,128)(2,1)S(1)}, u32[]{:S(2)}, u32[]{:S(2)}) %collective-permute-start.2) | collective-permute-done | bytes 16416 | tf_op jit(solution)/shard_map/ppermute | solution.py:17
  47.6 13.9 %while.18 = (s32[]{:T(128)}, f32[32,1024]{1,0:T(8,128)S(1)}, f32[32,1024]{1,0:T(8,128)S(1)}, bf16[32,1024]{1,0:T(8,128)(2,1)S(1)}, f32[8,8]{1,0:T(8,128)S(1)}, /...) while((s32[]{:T(128)}, f32[32,1024]{1,0:T(8,128)S(1)}, ...), condition=%wide.region_1.2_spmd.clone, body=%wide.region_0.1_spmd.clone.sunk | while | flops 24444952 | bytes 484844 | solution.py:123
  47.7 0.1 broadcast_bitcast_fusion.2
  47.8 0.8 fusion.44
  48.6 0.8 convolution_add_fusion.2
  49.4 0.1 broadcast_bitcast_fusion.2
  49.5 0.8 fusion.44
  50.3 0.8 convolution_add_fusion.2
  51.2 0.1 broadcast_bitcast_fusion.2
  51.3 0.8 fusion.44
  52.0 0.8 convolution_add_fusion.2
  52.9 0.1 broadcast_bitcast_fusion.2
  53.0 0.8 fusion.44
  53.8 0.8 convolution_add_fusion.2
  54.7 0.1 broadcast_bitcast_fusion.2
  54.8 0.8 fusion.44
  55.5 0.8 convolution_add_fusion.2
  56.4 0.1 broadcast_bitcast_fusion.2
  56.5 0.8 fusion.44
  57.3 0.8 convolution_add_fusion.2
  58.1 0.1 broadcast_bitcast_fusion.2
  58.2 0.8 fusion.44
  59.0 0.8 convolution_add_fusion.2
  59.9 0.1 broadcast_bitcast_fusion.2
  60.0 0.8 fusion.44
  60.7 0.8 convolution_add_fusion.2
  61.6 0.6 copy-done.2
  62.2 0.0 reduce-scatter.3.cloned.1.call-update
  62.2 0.0 reduce-scatter.5.cloned.1.call-start
  62.3 0.7 reduce-scatter.5.cloned.1.call-update
  63.1 0.8 fusion.23
  63.9 15.9 %reduce-scatter.3.cloned.1.call-done = f32[32,256]{1,0:T(8,128)} async-done(((f32[32,1024]{1,0:T(8,128)}), f32[32,256]{1,0:T(8,128)}) %reduce-scatter.3.cloned.1.call-update) | async-done | bytes 32784 | tf_op jit(solution)/shard_map/reduce_scatter | solution.py:124
  79.8 20.3 %reduce-scatter.5.cloned.1.call-done = f32[32,256]{1,0:T(8,128)} async-done(((f32[32,1024]{1,0:T(8,128)}), f32[32,256]{1,0:T(8,128)}) %reduce-scatter.5.cloned.1.call-update) | async-done | bytes 32784 | tf_op jit(solution)/shard_map/reduce_scatter | solution.py:125
  100.1 2.0 %multiply_reduce_fusion = (f32[256]{0:T(256)}, f32[32,256]{1,0:T(8,128)}, f32[32,256]{1,0:T(8,128)}) fusion(f32[32,256]{1,0:T(8,128)S(1)} %copy-done.3, f32[32,256]{1,0:T(8,128)} %reduce-scatter.3.cloned.1.call-done, f32[32,256]{1,0:T(8,128)S(1)} %fusion.23, f32[32,256]{1,0:T(8,128)} %reduce-scatter.5.cloned.1.call-done, f32[256]{0:T(256)S(1)} %broadcast_subtract_fusion, ...), kind=kLoop, calls=%fused_computation.46 | loop fusion | flops 57088 | bytes 199680 | tf_op jit(solution)/shard_map/reduce_sum | solution.py:133
  (62 shorter events, 0.4 us)
Async XLA Ops:
  7.2 55.8 %copy-start = (f32[32,2048]{1,0:T(8,128)S(1)}, f32[32,2048]{1,0:T(8,128)}, u32[]{:S(2)}) copy-start(f32[32,2048]{1,0:T(8,128)} %param.21) | copy-start | bytes 786436
  7.2 5.5 %copy-start.7 = (f32[2,256]{1,0:T(2,128)S(1)}, f32[2,256]{1,0:T(2,128)}, u32[]{:S(2)}) copy-start(f32[2,256]{1,0:T(2,128)} %param.13) | copy-start | bytes 6148
  7.2 5.5 %copy-start.4 = (f32[32,256]{1,0:T(8,128)S(1)}, f32[32,256]{1,0:T(8,128)}, u32[]{:S(2)}) copy-start(f32[32,256]{1,0:T(8,128)} %param.17) | copy-start | bytes 98308
  7.2 10.8 %copy-start.8 = (f32[256]{0:T(256)S(1)}, f32[256]{0:T(256)}, u32[]{:S(2)}) copy-start(f32[256]{0:T(256)} %param.14) | copy-start | bytes 3076
  7.2 10.8 %copy-start.6 = (f32[3,256]{1,0:T(4,128)S(1)}, f32[3,256]{1,0:T(4,128)}, u32[]{:S(2)}) copy-start(f32[3,256]{1,0:T(4,128)} %param.12) | copy-start | bytes 9220
  7.2 72.6 %reduce-scatter.3.cloned.1.call-start = ((), (), s32[]{:S(2)}) async-start(), calls=%async_computation.2 | async-start | bytes 163840 | tf_op jit(solution)/shard_map/reduce_scatter | solution.py:124
  8.8 27.8 %collective-permute-start = (bf16[32,256]{1,0:T(8,128)(2,1)S(1)}, bf16[32,256]{1,0:T(8,128)(2,1)S(1)}, u32[]{:S(2)}, u32[]{:S(2)}) collective-permute-start(bf16[32,256]{1,0:T(8,128)(2,1)S(1)} %get-tuple-element.259), channel_id=1, source_target_pairs={{0,4},{4,8},{8,12},{12,0},{1,5},{5,9},{9,13},{13,1},{2,6},{6,10},{... | collective-permute-start | bytes 49160 | tf_op jit(solution)/shard_map/ppermute | solution.py:17
  36.6 5.5 %collective-permute-start.1 = (bf16[32,256]{1,0:T(8,128)(2,1)S(1)}, bf16[32,256]{1,0:T(8,128)(2,1)S(1)}, u32[]{:S(2)}, u32[]{:S(2)}) collective-permute-start(bf16[32,256]{1,0:T(8,128)(2,1)S(1)} %collective-permute-done), channel_id=1, source_target_pairs={{0,4},{4,8},{8,12},{12,0},{1,5},{5,9},{9,13},{13,1},{2,6},{6,10},{... | collective-permute-start | bytes 49160 | tf_op jit(solution)/shard_map/ppermute | solution.py:17
  42.1 5.5 %collective-permute-start.2 = (bf16[32,256]{1,0:T(8,128)(2,1)S(1)}, bf16[32,256]{1,0:T(8,128)(2,1)S(1)}, u32[]{:S(2)}, u32[]{:S(2)}) collective-permute-start(bf16[32,256]{1,0:T(8,128)(2,1)S(1)} %collective-permute-done.1), channel_id=1, source_target_pairs={{0,4},{4,8},{8,12},{12,0},{1,5},{5,9},{9,13},{13,1},{2,6},{6,10},{... | collective-permute-start | bytes 49160 | tf_op jit(solution)/shard_map/ppermute | solution.py:17
  61.6 0.7 copy-start.2
  61.6 0.7 copy-start.1
  61.6 1.4 %copy-start.9 = (s32[2048]{0:T(1024)S(1)}, s32[2048]{0:T(1024)}, u32[]{:S(2)}) copy-start(s32[2048]{0:T(1024)} %param.20) | copy-start | bytes 24580
  62.2 37.9 %reduce-scatter.5.cloned.1.call-start = ((), (), s32[]{:S(2)}) async-start(), calls=%async_computation.3 | async-start | bytes 163840 | tf_op jit(solution)/shard_map/reduce_scatter | solution.py:125
  63.0 37.1 %copy-start.3 = (f32[32,256]{1,0:T(8,128)S(1)}, f32[32,256]{1,0:T(8,128)}, u32[]{:S(2)}) copy-start(f32[32,256]{1,0:T(8,128)} %param.16) | copy-start | bytes 98308
  63.0 37.1 %copy-start.5 = (f32[256]{0:T(256)S(1)}, f32[256]{0:T(256)}, u32[]{:S(2)}) copy-start(f32[256]{0:T(256)} %param.15) | copy-start | bytes 3076
Sparse Core Ops, SparseCore 0:
  62.4 17.3 reduce-scatter.2
  82.4 17.7 reduce-scatter.4
